TPU v7x, 32 devices: a whole 2x2x4 slice. The times are simulated.
32 devices in a mesh: tile: 8 (over y, x, core), trac: 4 (over z).
Axes of the slice: x: 2, y: 2, z: 4, core: 2. Of those that a mesh axis runs over, the one named last changes fastest.
Arguments:
- tracers: float32 [128, 512, 128], P(None, ('tile', 'trac')), may hold values from -6 to 6
- winds: float32 [2, 512, 128], P(None, ('tile', 'trac')), may hold values from -4 to 4
- chem_linear: float32 [128, 128], replicated, may hold values from -0.5 to 0.5
- chem_loss: float32 [128], replicated, may hold values from 0.5 to 4
- chem_left: float32 [4, 128, 128], replicated, may hold values from -0.25 to 0.25
- chem_right: float32 [4, 128, 128], replicated, may hold values from -0.25 to 0.25
- active_cells: int32 [32], P(('tile', 'trac')), may hold values from 256 to 2048
Outputs:
- tracers_out: float32 [128, 512, 128], P(None, ('tile', 'trac'))
- winds_out: float32 [2, 512, 128], P(None, ('tile', 'trac'))
Inputs may be any that keep to these rules, and one draw needn't show every extreme that they name: `active_cells`: active cells are the leading ones of the tile in row-major order.
All inputs are finite; a program needn't handle non-finite values.
Results may differ from a plain program's by a relative error of at most 0.0003.
Values sent between devices are 32-bit elements; how exact they have to be, the bound alone decides.
A program may use at most 64 MiB of HBM per device.

v0:
```python
import functools

import jax
import jax.numpy as jnp
from jax import lax
from jax.experimental import pallas as pl
from jax.experimental.pallas import tpu as pltpu
from jax.sharding import PartitionSpec as P

SUBS = 4
CHEM_STEPS = 3
WIND_STAGES = 3

DT_WIND = 0.1
VISCOSITY = 0.2
DT_TRACER = 0.1
DT_CHEM = 0.1

AXES = ("tile", "trac")
MESH = pl.DeviceIdType.MESH


def kernel(
    sizes,
    count_ref,
    tracers,
    winds,
    linear,
    loss,
    left,
    right,
    tracers_out,
    winds_out,
    lev,
    wind,
    wind_new,
    coef,
    lin_v,
    loss_v,
    fac_v,
    weights,
    done,
    row_sem,
    par_sem,
    wind_sem,
    out_sem,
    wout_sem,
    send_sem,
    recv_sem,
    wsend_sem,
    wrecv_sem,
):
    tiles, tracs = sizes
    species, rows, width = tracers.shape
    pairs = left.shape[0]
    depth = SUBS
    reach = SUBS + WIND_STAGES
    wrows = wind.shape[1]
    base = (wrows - rows) // 2
    shift = base - depth
    devices = tiles * tracs
    me = lax.axis_index(AXES[0]) * tracs + lax.axis_index(AXES[1])
    up_flat = lax.rem(me + 1, devices)
    down_flat = lax.rem(me + devices - 1, devices)
    up = (up_flat // tracs, lax.rem(up_flat, tracs))
    down = (down_flat // tracs, lax.rem(down_flat, tracs))

    barrier = pltpu.get_barrier_semaphore()
    for neighbour in (up, down):
        pl.semaphore_signal(barrier, inc=1, device_id=neighbour, device_id_type=MESH)

    order = []
    for k in range(depth):
        order += [rows - 1 - k, k]
    order += list(range(depth, rows - depth))

    def row_copy(r):
        return pltpu.make_async_copy(tracers.at[:, r, :], lev.at[0, depth + r], row_sem.at[r])

    own_wind = pltpu.make_async_copy(winds, wind.at[:, base : base + rows, :], wind_sem)
    own_wind.start()
    for r in order:
        row_copy(r).start()
    params = [
        pltpu.make_async_copy(linear, lin_v, par_sem.at[0]),
        pltpu.make_async_copy(loss, loss_v, par_sem.at[1]),
        pltpu.make_async_copy(left, fac_v.at[0], par_sem.at[2]),
        pltpu.make_async_copy(right, fac_v.at[1], par_sem.at[3]),
    ]
    for copy in params:
        copy.start()

    def wind_send(side):
        first = rows - reach if side == 0 else 0
        there = base - reach if side == 0 else base + rows
        return pltpu.make_async_remote_copy(
            src_ref=winds.at[:, first : first + reach, :],
            dst_ref=wind.at[:, there : there + reach, :],
            send_sem=wsend_sem.at[side],
            recv_sem=wrecv_sem.at[side],
            device_id=up if side == 0 else down,
            device_id_type=MESH,
        )

    def halo_send(side, k):
        here = depth + rows - 1 - k if side == 0 else depth + k
        there = depth - 1 - k if side == 0 else depth + rows + k
        return pltpu.make_async_remote_copy(
            src_ref=lev.at[0, here],
            dst_ref=lev.at[0, there],
            send_sem=send_sem.at[side, k],
            recv_sem=recv_sem.at[side, k],
            device_id=up if side == 0 else down,
            device_id_type=MESH,
        )

    pl.semaphore_wait(barrier, 2)
    for side in range(2):
        wind_send(side).start()
    for k in range(depth):
        row_copy(rows - 1 - k).wait()
        halo_send(0, k).start()
        row_copy(k).wait()
        halo_send(1, k).start()

    for copy in params:
        copy.wait()
    diag = lax.broadcasted_iota(jnp.int32, (species, species), 0) == lax.broadcasted_iota(
        jnp.int32, (species, species), 1
    )

    def put(slot, value):
        high = value.astype(jnp.bfloat16)
        low = (value - high.astype(jnp.float32)).astype(jnp.bfloat16)
        lines = pl.ds(slot * species, species)
        weights[lines, :species] = high
        weights[lines, species : 2 * species] = low

    put(0, DT_CHEM * (lin_v[...] - jnp.where(diag, loss_v[...], 0.0)))
    for p in range(pairs):
        put(1 + p, DT_CHEM * fac_v[0, p])
        put(1 + pairs + p, fac_v[1, p])

    for r in range(depth, rows - depth):
        row_copy(r).wait()
    own_wind.wait()
    for side in range(2):
        wind_send(side).wait()

    raw = wind[...]
    u0, v0 = raw[0], raw[1]

    def tendency(u, v):
        def of(f):
            east = pltpu.roll(f, width - 1, 1)
            west = pltpu.roll(f, 1, 1)
            north = pltpu.roll(f, wrows - 1, 0)
            south = pltpu.roll(f, 1, 0)
            along = (east - west) * 0.5
            across = (north - south) * 0.5
            spread = east + west + north + south - 4.0 * f
            return -(u * along + v * across) + VISCOSITY * spread

        return of(u), of(v)

    tu, tv = tendency(u0, v0)
    u1, v1 = u0 + DT_WIND * tu, v0 + DT_WIND * tv
    tu, tv = tendency(u1, v1)
    u2 = 0.75 * u0 + 0.25 * (u1 + DT_WIND * tu)
    v2 = 0.75 * v0 + 0.25 * (v1 + DT_WIND * tv)
    tu, tv = tendency(u2, v2)
    u3 = u0 / 3.0 + 2.0 / 3.0 * (u2 + DT_WIND * tu)
    v3 = v0 / 3.0 + 2.0 / 3.0 * (v2 + DT_WIND * tv)
    wind_new[0] = u3[base : base + rows]
    wind_new[1] = v3[base : base + rows]
    wind_copy = pltpu.make_async_copy(wind_new, winds_out, wout_sem)
    wind_copy.start()

    coef[0] = 1.0 - DT_TRACER * (jnp.abs(u3) + jnp.abs(v3))
    coef[1] = pltpu.roll(DT_TRACER * jnp.maximum(u3, 0.0), 1, 1)
    coef[2] = pltpu.roll(-DT_TRACER * jnp.minimum(u3, 0.0), width - 1, 1)
    coef[3] = pltpu.roll(DT_TRACER * jnp.maximum(v3, 0.0), 1, 0)
    coef[4] = pltpu.roll(-DT_TRACER * jnp.minimum(v3, 0.0), wrows - 1, 0)

    def advance(level, i):
        line = pl.ds(i + shift, 1)
        q = lev[level - 1, i]
        moved = coef[0, line, :] * q
        moved += coef[1, line, :] * pltpu.roll(q, 1, 1)
        moved += coef[2, line, :] * pltpu.roll(q, width - 1, 1)
        moved += coef[3, line, :] * lev[level - 1, i - 1]
        moved += coef[4, line, :] * lev[level - 1, i + 1]
        lev[level, i] = moved

    for level in range(1, depth + 1):

        @pl.loop(depth + level, depth + rows - level)
        def _(i, level=level):
            advance(level, i)

    count = count_ref[0]
    lane = lax.broadcasted_iota(jnp.int32, (1, width), 1)

    def react(first, second):
        conc = jnp.concatenate([lev[depth, first], lev[depth, second]], axis=1)
        cell = jnp.concatenate(
            [(first - depth) * width + lane, (second - depth) * width + lane], axis=1
        )
        mask = jnp.where(cell < count, 1.0, 0.0)
        for step in range(CHEM_STEPS):
            high = conc.astype(jnp.bfloat16)
            low = (conc - high.astype(jnp.float32)).astype(jnp.bfloat16)
            terms = jnp.dot(
                weights[...],
                jnp.concatenate([high, high], axis=0),
                preferred_element_type=jnp.float32,
            ) + jnp.dot(
                weights[...],
                jnp.concatenate([low, low], axis=0),
                preferred_element_type=jnp.float32,
            )
            rate = terms[:species]
            for p in range(pairs):
                one = (1 + p) * species
                two = (1 + pairs + p) * species
                rate += terms[one : one + species] * terms[two : two + species]
            conc = conc + rate * mask
        done[first - depth] = conc[:, :width]
        done[second - depth] = conc[:, width:]
        for i in (first, second):
            out_copy(i - depth).start()

    def out_copy(r):
        return pltpu.make_async_copy(done.at[r], tracers_out.at[:, r, :], out_sem.at[r])

    @pl.loop(0, (rows - 2 * depth) // 2)
    def _(i):
        react(2 * depth + 2 * i, 2 * depth + 2 * i + 1)

    @pl.loop(0, depth)
    def _(k):
        for side in range(2):
            halo_send(side, k).wait()
        for level in range(1, depth + 1):
            advance(level, depth - 1 - k + level)
            advance(level, depth + rows + k - level)
        react(2 * depth - 1 - k, rows + k)

    for r in range(rows):
        out_copy(r).wait()
    wind_copy.wait()


def on_device(sizes, tracers, winds, linear, loss, left, right, active):
    species, rows, width = tracers.shape
    pairs = left.shape[0]
    held = rows + 2 * SUBS
    wrows = rows + 2 * (-(-(SUBS + WIND_STAGES) // 8) * 8)
    f32 = jnp.float32
    dma = pltpu.SemaphoreType.DMA
    anywhere = pl.BlockSpec(memory_space=pl.ANY)
    return pl.pallas_call(
        functools.partial(kernel, sizes),
        out_shape=(
            jax.ShapeDtypeStruct(tracers.shape, f32),
            jax.ShapeDtypeStruct(winds.shape, f32),
        ),
        in_specs=[pl.BlockSpec(memory_space=pltpu.SMEM)] + [anywhere] * 6,
        out_specs=(anywhere, anywhere),
        scratch_shapes=[
            pltpu.VMEM((SUBS + 1, held, species, width), f32),
            pltpu.VMEM((2, wrows, width), f32),
            pltpu.VMEM(winds.shape, f32),
            pltpu.VMEM((5, wrows, width), f32),
            pltpu.VMEM(linear.shape, f32),
            pltpu.VMEM((1, species), f32),
            pltpu.VMEM((2,) + left.shape, f32),
            pltpu.VMEM(((1 + 2 * pairs) * species, 2 * species), jnp.bfloat16),
            pltpu.VMEM((rows, species, width), f32),
            dma((rows,)),
            dma((4,)),
            dma,
            dma((rows,)),
            dma,
            dma((2, SUBS)),
            dma((2, SUBS)),
            dma((2,)),
            dma((2,)),
        ],
        compiler_params=pltpu.CompilerParams(collective_id=0, has_side_effects=True),
    )(active, tracers, winds, linear, loss.reshape(1, species), left, right)


def solution(mesh):
    sizes = tuple(mesh.shape[axis] for axis in AXES)
    banded = P(None, AXES, None)
    return jax.shard_map(
        functools.partial(on_device, sizes),
        mesh=mesh,
        in_specs=(banded, banded, P(), P(), P(), P(), P(AXES)),
        out_specs=(banded, banded),
        check_vma=False,
    )
```

profile of v0, /device:TPU:0, one launch (start us, length us, event | category | flops | bytes accessed | tf_op | source)
XLA Modules:
  0.0 37.8 jit_solution(11358761157919893447)
XLA Ops:
  1.3 33.6 %shard_map.86 = (f32[128,16,128]{2,1,0:T(8,128)}, f32[2,16,128]{2,1,0:T(8,128)}) custom-call(s32[1]{0:T(128)S(6)} %copy.11.count_ref, f32[128,16,128]{2,1,0:T(8,128)} %tracers.1, f32[2,16,128]{2,1,0:T(8,128)} %winds.1, f32[128,128]{1,0:T(8,128)} %linear.1, f32[1,128]{1,0:T(1,128)} %bitcast.1, f32[4,128,128]{2,1,0:T(8,128)} %left.1, f32[4,128,128]{2,1,0:T(8,128)} %right.1), custom_call_target="tpu_custom_call" | custom-call | tf_op jit(solution)/shard_map/pallas_call | solution.py:262
  34.9 0.0 copy-start
  34.9 2.3 %copy.12 = f32[128,16,128]{2,1,0:T(8,128)} copy(f32[128,16,128]{2,1,0:T(8,128)} %get-tuple-element.4) | data formatting | bytes 2097152
  37.2 0.0 copy-done
  37.2 0.6 %copy.13 = f32[2,16,128]{2,1,0:T(8,128)} copy(f32[2,16,128]{2,1,0:T(8,128)S(1)} %copy-done) | data formatting | bytes 32768
Async XLA Ops:
  34.9 2.3 %copy-start = (f32[2,16,128]{2,1,0:T(8,128)S(1)}, f32[2,16,128]{2,1,0:T(8,128)}, u32[]{:S(2)}) copy-start(f32[2,16,128]{2,1,0:T(8,128)} %get-tuple-element.5) | copy-start | bytes 49156
where the time goes:
time: 38 us; the launch traced here: 37.8 us
  Pallas kernels  33.6 us (88%)
  local copies, waits for them, and re-layouts  2.88 us (8%)
  between operations  1.3 us (3%)
    pallas_call x1, Pallas kernels, on_device(): pl.pallas_call(functools.partial(kernel, sizes), out_shape=(jax.ShapeDtyp...  33.6 us
    unnamed x4, local copies, waits for them, and re-layouts  2.88 us

commit v1 on v0

--- a/solution.py
+++ b/solution.py
@@ -29,22 +29,18 @@
     loss,
     left,
     right,
-    tracers_out,
-    winds_out,
+    done,
+    wind_new,
     lev,
     wind,
-    wind_new,
     coef,
     lin_v,
     loss_v,
     fac_v,
     weights,
-    done,
     row_sem,
     par_sem,
     wind_sem,
-    out_sem,
-    wout_sem,
     send_sem,
     recv_sem,
     wsend_sem,
@@ -114,14 +110,16 @@
             device_id_type=MESH,
         )
 
+    def edge_send(side, k):
+        row_copy(rows - 1 - k if side == 0 else k).wait()
+        halo_send(side, k).start()
+
     pl.semaphore_wait(barrier, 2)
     for side in range(2):
         wind_send(side).start()
     for k in range(depth):
-        row_copy(rows - 1 - k).wait()
-        halo_send(0, k).start()
-        row_copy(k).wait()
-        halo_send(1, k).start()
+        for side in range(2):
+            edge_send(side, k)
 
     for copy in params:
         copy.wait()
@@ -144,43 +142,41 @@
     for r in range(depth, rows - depth):
         row_copy(r).wait()
     own_wind.wait()
-    for side in range(2):
-        wind_send(side).wait()
-
-    raw = wind[...]
-    u0, v0 = raw[0], raw[1]
-
-    def tendency(u, v):
-        def of(f):
-            east = pltpu.roll(f, width - 1, 1)
-            west = pltpu.roll(f, 1, 1)
-            north = pltpu.roll(f, wrows - 1, 0)
-            south = pltpu.roll(f, 1, 0)
-            along = (east - west) * 0.5
-            across = (north - south) * 0.5
-            spread = east + west + north + south - 4.0 * f
-            return -(u * along + v * across) + VISCOSITY * spread
-
-        return of(u), of(v)
-
-    tu, tv = tendency(u0, v0)
-    u1, v1 = u0 + DT_WIND * tu, v0 + DT_WIND * tv
-    tu, tv = tendency(u1, v1)
-    u2 = 0.75 * u0 + 0.25 * (u1 + DT_WIND * tu)
-    v2 = 0.75 * v0 + 0.25 * (v1 + DT_WIND * tv)
-    tu, tv = tendency(u2, v2)
-    u3 = u0 / 3.0 + 2.0 / 3.0 * (u2 + DT_WIND * tu)
-    v3 = v0 / 3.0 + 2.0 / 3.0 * (v2 + DT_WIND * tv)
-    wind_new[0] = u3[base : base + rows]
-    wind_new[1] = v3[base : base + rows]
-    wind_copy = pltpu.make_async_copy(wind_new, winds_out, wout_sem)
-    wind_copy.start()
-
-    coef[0] = 1.0 - DT_TRACER * (jnp.abs(u3) + jnp.abs(v3))
-    coef[1] = pltpu.roll(DT_TRACER * jnp.maximum(u3, 0.0), 1, 1)
-    coef[2] = pltpu.roll(-DT_TRACER * jnp.minimum(u3, 0.0), width - 1, 1)
-    coef[3] = pltpu.roll(DT_TRACER * jnp.maximum(v3, 0.0), 1, 0)
-    coef[4] = pltpu.roll(-DT_TRACER * jnp.minimum(v3, 0.0), wrows - 1, 0)
+
+    def update_winds(lines):
+        raw = wind[:, lines]
+        u0, v0 = raw[0], raw[1]
+        held = u0.shape[0]
+
+        def tendency(u, v):
+            def of(f):
+                east = pltpu.roll(f, width - 1, 1)
+                west = pltpu.roll(f, 1, 1)
+                north = pltpu.roll(f, held - 1, 0)
+                south = pltpu.roll(f, 1, 0)
+                along = (east - west) * 0.5
+                across = (north - south) * 0.5
+                spread = east + west + north + south - 4.0 * f
+                return -(u * along + v * across) + VISCOSITY * spread
+
+            return of(u), of(v)
+
+        tu, tv = tendency(u0, v0)
+        u1, v1 = u0 + DT_WIND * tu, v0 + DT_WIND * tv
+        tu, tv = tendency(u1, v1)
+        u2 = 0.75 * u0 + 0.25 * (u1 + DT_WIND * tu)
+        v2 = 0.75 * v0 + 0.25 * (v1 + DT_WIND * tv)
+        tu, tv = tendency(u2, v2)
+        u3 = u0 / 3.0 + 2.0 / 3.0 * (u2 + DT_WIND * tu)
+        v3 = v0 / 3.0 + 2.0 / 3.0 * (v2 + DT_WIND * tv)
+        if held == wrows:
+            wind_new[0] = u3[base : base + rows]
+            wind_new[1] = v3[base : base + rows]
+        coef[0, lines] = 1.0 - DT_TRACER * (jnp.abs(u3) + jnp.abs(v3))
+        coef[1, lines] = pltpu.roll(DT_TRACER * jnp.maximum(u3, 0.0), 1, 1)
+        coef[2, lines] = pltpu.roll(-DT_TRACER * jnp.minimum(u3, 0.0), width - 1, 1)
+        coef[3, lines] = pltpu.roll(DT_TRACER * jnp.maximum(v3, 0.0), 1, 0)
+        coef[4, lines] = pltpu.roll(-DT_TRACER * jnp.minimum(v3, 0.0), held - 1, 0)
 
     def advance(level, i):
         line = pl.ds(i + shift, 1)
@@ -192,10 +188,9 @@
         moved += coef[4, line, :] * lev[level - 1, i + 1]
         lev[level, i] = moved
 
-    for level in range(1, depth + 1):
-
-        @pl.loop(depth + level, depth + rows - level)
-        def _(i, level=level):
+    def sweep(level, first, last):
+        @pl.loop(first, last)
+        def _(i):
             advance(level, i)
 
     count = count_ref[0]
@@ -227,28 +222,43 @@
             conc = conc + rate * mask
         done[first - depth] = conc[:, :width]
         done[second - depth] = conc[:, width:]
-        for i in (first, second):
-            out_copy(i - depth).start()
-
-    def out_copy(r):
-        return pltpu.make_async_copy(done.at[r], tracers_out.at[:, r, :], out_sem.at[r])
-
-    @pl.loop(0, (rows - 2 * depth) // 2)
+
+    update_winds(slice(base, base + rows))
+    low, high = depth, depth + rows
+    for level in range(1, depth + 1):
+        sweep(level, low + WIND_STAGES + level, high - WIND_STAGES - level)
+    middle = range(low + reach, high - reach, 2)
+    for i in middle:
+        react(i, i + 1)
+
+    for side in range(2):
+        wind_send(side).wait()
+    update_winds(slice(0, wrows))
+    for level in range(1, depth + 1):
+        sweep(level, low + level, low + WIND_STAGES + level)
+        sweep(level, high - WIND_STAGES - level, high - level)
+
+    @pl.loop(0, WIND_STAGES)
     def _(i):
-        react(2 * depth + 2 * i, 2 * depth + 2 * i + 1)
-
-    @pl.loop(0, depth)
-    def _(k):
+        react(low + depth + i, high - depth - 1 - i)
+
+    for k in range(depth):
         for side in range(2):
             halo_send(side, k).wait()
         for level in range(1, depth + 1):
-            advance(level, depth - 1 - k + level)
-            advance(level, depth + rows + k - level)
-        react(2 * depth - 1 - k, rows + k)
-
-    for r in range(rows):
-        out_copy(r).wait()
-    wind_copy.wait()
+            advance(level, low - 1 - k + level)
+            advance(level, high + k - level)
+        react(low + depth - 1 - k, high - depth + k)
+
+
+def finish(done, wind_new, tracers_out, winds_out, out_sem, wind_sem):
+    copies = [pltpu.make_async_copy(wind_new, winds_out, wind_sem)]
+    for r in range(done.shape[0]):
+        copies.append(pltpu.make_async_copy(done.at[r], tracers_out.at[:, r, :], out_sem.at[r]))
+    for copy in copies:
+        copy.start()
+    for copy in copies:
+        copy.wait()
 
 
 def on_device(sizes, tracers, winds, linear, loss, left, right, active):
@@ -259,28 +269,25 @@
     f32 = jnp.float32
     dma = pltpu.SemaphoreType.DMA
     anywhere = pl.BlockSpec(memory_space=pl.ANY)
-    return pl.pallas_call(
+    vmem = pl.BlockSpec(memory_space=pltpu.VMEM)
+    done, wind_new = pl.pallas_call(
         functools.partial(kernel, sizes),
         out_shape=(
-            jax.ShapeDtypeStruct(tracers.shape, f32),
-            jax.ShapeDtypeStruct(winds.shape, f32),
+            pltpu.VMEM((rows, species, width), f32),
+            pltpu.VMEM(winds.shape, f32),
         ),
         in_specs=[pl.BlockSpec(memory_space=pltpu.SMEM)] + [anywhere] * 6,
-        out_specs=(anywhere, anywhere),
+        out_specs=(vmem, vmem),
         scratch_shapes=[
             pltpu.VMEM((SUBS + 1, held, species, width), f32),
             pltpu.VMEM((2, wrows, width), f32),
-            pltpu.VMEM(winds.shape, f32),
             pltpu.VMEM((5, wrows, width), f32),
             pltpu.VMEM(linear.shape, f32),
             pltpu.VMEM((1, species), f32),
             pltpu.VMEM((2,) + left.shape, f32),
             pltpu.VMEM(((1 + 2 * pairs) * species, 2 * species), jnp.bfloat16),
-            pltpu.VMEM((rows, species, width), f32),
             dma((rows,)),
             dma((4,)),
-            dma,
-            dma((rows,)),
             dma,
             dma((2, SUBS)),
             dma((2, SUBS)),
@@ -289,6 +296,19 @@
         ],
         compiler_params=pltpu.CompilerParams(collective_id=0, has_side_effects=True),
     )(active, tracers, winds, linear, loss.reshape(1, species), left, right)
+    return pl.pallas_call(
+        finish,
+        out_shape=(
+            jax.ShapeDtypeStruct(tracers.shape, f32),
+            jax.ShapeDtypeStruct(winds.shape, f32),
+        ),
+        in_specs=[vmem, vmem],
+        out_specs=(anywhere, anywhere),
+        scratch_shapes=[dma((rows,)), dma],
+    )(
+        pltpu.with_memory_space_constraint(done, pltpu.VMEM),
+        pltpu.with_memory_space_constraint(wind_new, pltpu.VMEM),
+    )
 
 
 def solution(mesh):

time: 38 us -> 33.2 us (0.87)
  local copies, waits for them, and re-layouts: 2.88 us -> 0 us
  Pallas kernels: 33.6 us -> 31.7 us
    unnamed x4 -> x0, local copies, waits for them, and re-layouts: 2.88 us -> none
    pallas_call x1 -> x2, Pallas kernels: 33.6 us -> 31.7 us  [the longest x1 30.6 us: on_device(): pl.pallas_call(functools.partial(kernel, sizes), out_shape=(pltpu.VMEM((r...]
where the time goes in v1:
time: 33.2 us; the launch traced here: 33 us
  Pallas kernels  31.7 us (95%)
  between operations  1.29 us (4%)
    pallas_call x1, Pallas kernels, on_device(): pl.pallas_call(functools.partial(kernel, sizes), out_shape=(pltpu.VMEM((r...  30.6 us
    pallas_call x1, Pallas kernels, on_device(): pl.pallas_call(finish, out_shape=(jax.ShapeDtypeStruct(tracers.shape, f32...  1.11 us

profile of v1, /device:TPU:0, one launch (start us, length us, event | category | flops | bytes accessed | tf_op | source)
XLA Modules:
  0.0 33.0 jit_solution(7529814185169645542)
XLA Ops:
  1.3 30.6 %shard_map.86 = (f32[16,128,128]{2,1,0:T(8,128)S(1)}, f32[2,16,128]{2,1,0:T(8,128)S(1)}) custom-call(s32[1]{0:T(128)S(6)} %copy.9.count_ref, f32[128,16,128]{2,1,0:T(8,128)} %tracers.1, f32[2,16,128]{2,1,0:T(8,128)} %winds.1, f32[128,128]{1,0:T(8,128)} %linear.1, f32[1,128]{1,0:T(1,128)} %bitcast.1, f32[4,128,128]{2,1,0:T(8,128)} %left.1, f32[4,128,128]{2,1,0:T(8,128)} %right.1), custom_call_target="tpu_custom_call" | custom-call | tf_op jit(solution)/shard_map/pallas_call | solution.py:273
  31.9 1.1 %shard_map.87 = (f32[128,16,128]{2,1,0:T(8,128)}, f32[2,16,128]{2,1,0:T(8,128)}) custom-call(f32[16,128,128]{2,1,0:T(8,128)S(1)} %get-tuple-element.4.done, f32[2,16,128]{2,1,0:T(8,128)S(1)} %get-tuple-element.5.wind_new), custom_call_target="tpu_custom_call" | custom-call | tf_op jit(solution)/shard_map/pallas_call | solution.py:299

commit v2 on v1

--- a/solution.py
+++ b/solution.py
@@ -110,16 +110,19 @@
             device_id_type=MESH,
         )
 
-    def edge_send(side, k):
-        row_copy(rows - 1 - k if side == 0 else k).wait()
-        halo_send(side, k).start()
-
-    pl.semaphore_wait(barrier, 2)
-    for side in range(2):
-        wind_send(side).start()
-    for k in range(depth):
+    def send_all():
+        pl.semaphore_wait(barrier, 2)
         for side in range(2):
-            edge_send(side, k)
+            wind_send(side).start()
+        for k in range(depth):
+            for side in range(2):
+                halo_send(side, k).start()
+
+    place = lax.axis_index(AXES[1])
+    inside = jnp.logical_and(place > 0, place < tracs - 1)
+    for r in order[: 2 * depth]:
+        row_copy(r).wait()
+    pl.when(inside)(send_all)
 
     for copy in params:
         copy.wait()
@@ -196,32 +199,37 @@
     count = count_ref[0]
     lane = lax.broadcasted_iota(jnp.int32, (1, width), 1)
 
-    def react(first, second):
-        conc = jnp.concatenate([lev[depth, first], lev[depth, second]], axis=1)
-        cell = jnp.concatenate(
-            [(first - depth) * width + lane, (second - depth) * width + lane], axis=1
-        )
-        mask = jnp.where(cell < count, 1.0, 0.0)
+    def react(*couples):
+        concs, masks = [], []
+        for first, second in couples:
+            concs.append(jnp.concatenate([lev[depth, first], lev[depth, second]], axis=1))
+            cell = jnp.concatenate(
+                [(first - depth) * width + lane, (second - depth) * width + lane], axis=1
+            )
+            masks.append(jnp.where(cell < count, 1.0, 0.0))
         for step in range(CHEM_STEPS):
-            high = conc.astype(jnp.bfloat16)
-            low = (conc - high.astype(jnp.float32)).astype(jnp.bfloat16)
-            terms = jnp.dot(
-                weights[...],
-                jnp.concatenate([high, high], axis=0),
-                preferred_element_type=jnp.float32,
-            ) + jnp.dot(
-                weights[...],
-                jnp.concatenate([low, low], axis=0),
-                preferred_element_type=jnp.float32,
-            )
-            rate = terms[:species]
-            for p in range(pairs):
-                one = (1 + p) * species
-                two = (1 + pairs + p) * species
-                rate += terms[one : one + species] * terms[two : two + species]
-            conc = conc + rate * mask
-        done[first - depth] = conc[:, :width]
-        done[second - depth] = conc[:, width:]
+            for j, mask in enumerate(masks):
+                conc = concs[j]
+                high = conc.astype(jnp.bfloat16)
+                low = (conc - high.astype(jnp.float32)).astype(jnp.bfloat16)
+                terms = jnp.dot(
+                    weights[...],
+                    jnp.concatenate([high, high], axis=0),
+                    preferred_element_type=jnp.float32,
+                ) + jnp.dot(
+                    weights[...],
+                    jnp.concatenate([low, low], axis=0),
+                    preferred_element_type=jnp.float32,
+                )
+                rate = terms[:species]
+                for p in range(pairs):
+                    one = (1 + p) * species
+                    two = (1 + pairs + p) * species
+                    rate += terms[one : one + species] * terms[two : two + species]
+                concs[j] = conc + rate * mask
+        for (first, second), conc in zip(couples, concs):
+            done[first - depth] = conc[:, :width]
+            done[second - depth] = conc[:, width:]
 
     update_winds(slice(base, base + rows))
     low, high = depth, depth + rows
@@ -229,7 +237,9 @@
         sweep(level, low + WIND_STAGES + level, high - WIND_STAGES - level)
     middle = range(low + reach, high - reach, 2)
     for i in middle:
-        react(i, i + 1)
+        react((i, i + 1))
+
+    pl.when(jnp.logical_not(inside))(send_all)
 
     for side in range(2):
         wind_send(side).wait()
@@ -238,17 +248,21 @@
         sweep(level, low + level, low + WIND_STAGES + level)
         sweep(level, high - WIND_STAGES - level, high - level)
 
-    @pl.loop(0, WIND_STAGES)
-    def _(i):
-        react(low + depth + i, high - depth - 1 - i)
-
-    for k in range(depth):
+    def edge(k):
         for side in range(2):
             halo_send(side, k).wait()
         for level in range(1, depth + 1):
             advance(level, low - 1 - k + level)
             advance(level, high + k - level)
-        react(low + depth - 1 - k, high - depth + k)
+
+    couples = [(low + depth + i, high - depth - 1 - i) for i in reversed(range(-depth, WIND_STAGES))]
+    ready = WIND_STAGES
+    for at in range(0, len(couples), 2):
+        batch = couples[at : at + 2]
+        while ready < at + len(batch):
+            edge(ready - WIND_STAGES)
+            ready += 1
+        react(*batch)
 
 
 def finish(done, wind_new, tracers_out, winds_out, out_sem, wind_sem):

time: 33.2 us -> 30.8 us (0.928)
  Pallas kernels: 31.7 us -> 29.3 us
    pallas_call x1, Pallas kernels: 30.6 us -> 28.2 us  [on_device(): pl.pallas_call(functools.partial(kernel, sizes), out_shape=(pltpu.VMEM((r...]
where the time goes in v2:
time: 30.8 us; the launch traced here: 30.6 us
  Pallas kernels  29.3 us (95%)
  between operations  1.29 us (4%)
    pallas_call x1, Pallas kernels, on_device(): pl.pallas_call(functools.partial(kernel, sizes), out_shape=(pltpu.VMEM((r...  28.2 us
    pallas_call x1, Pallas kernels, on_device(): pl.pallas_call(finish, out_shape=(jax.ShapeDtypeStruct(tracers.shape, f32...  1.11 us

profile of v2, /device:TPU:0, one launch (start us, length us, event | category | flops | bytes accessed | tf_op | source)
XLA Modules:
  0.0 30.6 jit_solution(1650885063804350306)
XLA Ops:
  1.3 28.2 %shard_map.86 = (f32[16,128,128]{2,1,0:T(8,128)S(1)}, f32[2,16,128]{2,1,0:T(8,128)S(1)}) custom-call(s32[1]{0:T(128)S(6)} %copy.9.count_ref, f32[128,16,128]{2,1,0:T(8,128)} %tracers.1, f32[2,16,128]{2,1,0:T(8,128)} %winds.1, f32[128,128]{1,0:T(8,128)} %linear.1, f32[1,128]{1,0:T(1,128)} %bitcast.1, f32[4,128,128]{2,1,0:T(8,128)} %left.1, f32[4,128,128]{2,1,0:T(8,128)} %right.1), custom_call_target="tpu_custom_call" | custom-call | tf_op jit(solution)/shard_map/pallas_call | solution.py:287
  29.5 1.1 %shard_map.87 = (f32[128,16,128]{2,1,0:T(8,128)}, f32[2,16,128]{2,1,0:T(8,128)}) custom-call(f32[16,128,128]{2,1,0:T(8,128)S(1)} %get-tuple-element.4.done, f32[2,16,128]{2,1,0:T(8,128)S(1)} %get-tuple-element.5.wind_new), custom_call_target="tpu_custom_call" | custom-call | tf_op jit(solution)/shard_map/pallas_call | solution.py:313

commit v3 on v2

--- a/solution.py
+++ b/solution.py
@@ -10,6 +10,8 @@
 SUBS = 4
 CHEM_STEPS = 3
 WIND_STAGES = 3
+PARTS = 2
+BATCH = 1
 
 DT_WIND = 0.1
 VISCOSITY = 0.2
@@ -130,12 +132,17 @@
         jnp.int32, (species, species), 1
     )
 
+    block = species // PARTS
+    height = (1 + 2 * pairs) * block
+
     def put(slot, value):
         high = value.astype(jnp.bfloat16)
         low = (value - high.astype(jnp.float32)).astype(jnp.bfloat16)
-        lines = pl.ds(slot * species, species)
-        weights[lines, :species] = high
-        weights[lines, species : 2 * species] = low
+        for part in range(PARTS):
+            lines = pl.ds((part * (1 + 2 * pairs) + slot) * block, block)
+            own = slice(part * block, (part + 1) * block)
+            weights[lines, :species] = high[own]
+            weights[lines, species : 2 * species] = low[own]
 
     put(0, DT_CHEM * (lin_v[...] - jnp.where(diag, loss_v[...], 0.0)))
     for p in range(pairs):
@@ -212,21 +219,21 @@
                 conc = concs[j]
                 high = conc.astype(jnp.bfloat16)
                 low = (conc - high.astype(jnp.float32)).astype(jnp.bfloat16)
-                terms = jnp.dot(
-                    weights[...],
-                    jnp.concatenate([high, high], axis=0),
-                    preferred_element_type=jnp.float32,
-                ) + jnp.dot(
-                    weights[...],
-                    jnp.concatenate([low, low], axis=0),
-                    preferred_element_type=jnp.float32,
-                )
-                rate = terms[:species]
-                for p in range(pairs):
-                    one = (1 + p) * species
-                    two = (1 + pairs + p) * species
-                    rate += terms[one : one + species] * terms[two : two + species]
-                concs[j] = conc + rate * mask
+                high = jnp.concatenate([high, high], axis=0)
+                low = jnp.concatenate([low, low], axis=0)
+                blocks = []
+                for part in range(PARTS):
+                    lhs = weights[part * height : (part + 1) * height]
+                    terms = jnp.dot(lhs, high, preferred_element_type=jnp.float32) + jnp.dot(
+                        lhs, low, preferred_element_type=jnp.float32
+                    )
+                    rate = terms[:block]
+                    for p in range(pairs):
+                        one = (1 + p) * block
+                        two = (1 + pairs + p) * block
+                        rate += terms[one : one + block] * terms[two : two + block]
+                    blocks.append(conc[part * block : (part + 1) * block] + rate * mask)
+                concs[j] = jnp.concatenate(blocks, axis=0)
         for (first, second), conc in zip(couples, concs):
             done[first - depth] = conc[:, :width]
             done[second - depth] = conc[:, width:]
@@ -257,8 +264,8 @@
 
     couples = [(low + depth + i, high - depth - 1 - i) for i in reversed(range(-depth, WIND_STAGES))]
     ready = WIND_STAGES
-    for at in range(0, len(couples), 2):
-        batch = couples[at : at + 2]
+    for at in range(0, len(couples), BATCH):
+        batch = couples[at : at + BATCH]
         while ready < at + len(batch):
             edge(ready - WIND_STAGES)
             ready += 1

time: 30.8 us -> 30.5 us (level)
    pallas_call x1, Pallas kernels: 28.2 us -> 27.9 us  [on_device(): pl.pallas_call(functools.partial(kernel, sizes), out_shape=(pltpu.VMEM((r...]
where the time goes in v3:
time: 30.5 us; the launch traced here: 30.3 us
  Pallas kernels  29 us (95%)
  between operations  1.29 us (4%)
    pallas_call x1, Pallas kernels, on_device(): pl.pallas_call(functools.partial(kernel, sizes), out_shape=(pltpu.VMEM((r...  27.9 us
    pallas_call x1, Pallas kernels, on_device(): pl.pallas_call(finish, out_shape=(jax.ShapeDtypeStruct(tracers.shape, f32...  1.11 us

profile of v3, /device:TPU:0, one launch (start us, length us, event | category | flops | bytes accessed | tf_op | source)
XLA Modules:
  0.0 30.3 jit_solution(1022880595248192682)
XLA Ops:
  1.3 27.9 %shard_map.86 = (f32[16,128,128]{2,1,0:T(8,128)S(1)}, f32[2,16,128]{2,1,0:T(8,128)S(1)}) custom-call(s32[1]{0:T(128)S(6)} %copy.9.count_ref, f32[128,16,128]{2,1,0:T(8,128)} %tracers.1, f32[2,16,128]{2,1,0:T(8,128)} %winds.1, f32[128,128]{1,0:T(8,128)} %linear.1, f32[1,128]{1,0:T(1,128)} %bitcast.1, f32[4,128,128]{2,1,0:T(8,128)} %left.1, f32[4,128,128]{2,1,0:T(8,128)} %right.1), custom_call_target="tpu_custom_call" | custom-call | tf_op jit(solution)/shard_map/pallas_call | solution.py:294
  29.2 1.1 %shard_map.87 = (f32[128,16,128]{2,1,0:T(8,128)}, f32[2,16,128]{2,1,0:T(8,128)}) custom-call(f32[16,128,128]{2,1,0:T(8,128)S(1)} %get-tuple-element.4.done, f32[2,16,128]{2,1,0:T(8,128)S(1)} %get-tuple-element.5.wind_new), custom_call_target="tpu_custom_call" | custom-call | tf_op jit(solution)/shard_map/pallas_call | solution.py:320

commit v4 on v3

--- a/solution.py
+++ b/solution.py
@@ -11,6 +11,7 @@
 CHEM_STEPS = 3
 WIND_STAGES = 3
 PARTS = 2
+LEAD = 2
 BATCH = 1
 
 DT_WIND = 0.1
@@ -112,19 +113,31 @@
             device_id_type=MESH,
         )
 
-    def send_all():
-        pl.semaphore_wait(barrier, 2)
+    for r in order[: 2 * depth]:
+        row_copy(r).wait()
+    pl.semaphore_wait(barrier, 2)
+    place = lax.axis_index(AXES[1])
+    last = tracs - 1
+
+    @pl.when(jnp.logical_and(place > 0, place < last))
+    def _():
         for side in range(2):
             wind_send(side).start()
         for k in range(depth):
             for side in range(2):
                 halo_send(side, k).start()
 
-    place = lax.axis_index(AXES[1])
-    inside = jnp.logical_and(place > 0, place < tracs - 1)
-    for r in order[: 2 * depth]:
-        row_copy(r).wait()
-    pl.when(inside)(send_all)
+    for end, near in ((0, 0), (last, 1)):
+
+        @pl.when(place == end)
+        def _(near=near):
+            wind_send(1 - near).start()
+            wind_send(near).start()
+            for k in range(depth + LEAD):
+                if k < depth:
+                    halo_send(1 - near, k).start()
+                if k >= LEAD:
+                    halo_send(near, k - LEAD).start()
 
     for copy in params:
         copy.wait()
@@ -245,8 +258,6 @@
     middle = range(low + reach, high - reach, 2)
     for i in middle:
         react((i, i + 1))
-
-    pl.when(jnp.logical_not(inside))(send_all)
 
     for side in range(2):
         wind_send(side).wait()

time: 30.5 us -> 27.2 us (0.89)
  Pallas kernels: 29 us -> 25.8 us
    pallas_call x1, Pallas kernels: 27.9 us -> 24.7 us  [on_device(): pl.pallas_call(functools.partial(kernel, sizes), out_shape=(pltpu.VMEM((r...]
where the time goes in v4:
time: 27.2 us; the launch traced here: 27.1 us
  Pallas kernels  25.8 us (95%)
  between operations  1.29 us (5%)
    pallas_call x1, Pallas kernels, on_device(): pl.pallas_call(functools.partial(kernel, sizes), out_shape=(pltpu.VMEM((r...  24.7 us
    pallas_call x1, Pallas kernels, on_device(): pl.pallas_call(finish, out_shape=(jax.ShapeDtypeStruct(tracers.shape, f32...  1.11 us

profile of v4, /device:TPU:0, one launch (start us, length us, event | category | flops | bytes accessed | tf_op | source)
XLA Modules:
  0.0 27.1 jit_solution(9269851069001767746)
XLA Ops:
  1.3 24.7 %shard_map.86 = (f32[16,128,128]{2,1,0:T(8,128)S(1)}, f32[2,16,128]{2,1,0:T(8,128)S(1)}) custom-call(s32[1]{0:T(128)S(6)} %copy.9.count_ref, f32[128,16,128]{2,1,0:T(8,128)} %tracers.1, f32[2,16,128]{2,1,0:T(8,128)} %winds.1, f32[128,128]{1,0:T(8,128)} %linear.1, f32[1,128]{1,0:T(1,128)} %bitcast.1, f32[4,128,128]{2,1,0:T(8,128)} %left.1, f32[4,128,128]{2,1,0:T(8,128)} %right.1), custom_call_target="tpu_custom_call" | custom-call | tf_op jit(solution)/shard_map/pallas_call | solution.py:305
  26.0 1.1 %shard_map.87 = (f32[128,16,128]{2,1,0:T(8,128)}, f32[2,16,128]{2,1,0:T(8,128)}) custom-call(f32[16,128,128]{2,1,0:T(8,128)S(1)} %get-tuple-element.4.done, f32[2,16,128]{2,1,0:T(8,128)S(1)} %get-tuple-element.5.wind_new), custom_call_target="tpu_custom_call" | custom-call | tf_op jit(solution)/shard_map/pallas_call | solution.py:331

commit v5 on v4

--- a/solution.py
+++ b/solution.py
@@ -43,6 +43,8 @@
     weights,
     row_sem,
     par_sem,
+    count_v,
+    count_sem,
     wind_sem,
     send_sem,
     recv_sem,
@@ -78,6 +80,8 @@
 
     own_wind = pltpu.make_async_copy(winds, wind.at[:, base : base + rows, :], wind_sem)
     own_wind.start()
+    count_copy = pltpu.make_async_copy(count_ref, count_v, count_sem)
+    count_copy.start()
     for r in order:
         row_copy(r).start()
     params = [
@@ -216,7 +220,8 @@
         def _(i):
             advance(level, i)
 
-    count = count_ref[0]
+    count_copy.wait()
+    count = count_v[0]
     lane = lax.broadcasted_iota(jnp.int32, (1, width), 1)
 
     def react(*couples):
@@ -267,10 +272,11 @@
         sweep(level, high - WIND_STAGES - level, high - level)
 
     def edge(k):
-        for side in range(2):
-            halo_send(side, k).wait()
+        halo_send(0, k).wait()
         for level in range(1, depth + 1):
             advance(level, low - 1 - k + level)
+        halo_send(1, k).wait()
+        for level in range(1, depth + 1):
             advance(level, high + k - level)
 
     couples = [(low + depth + i, high - depth - 1 - i) for i in reversed(range(-depth, WIND_STAGES))]
@@ -308,7 +314,7 @@
             pltpu.VMEM((rows, species, width), f32),
             pltpu.VMEM(winds.shape, f32),
         ),
-        in_specs=[pl.BlockSpec(memory_space=pltpu.SMEM)] + [anywhere] * 6,
+        in_specs=[pl.BlockSpec(memory_space=pltpu.HBM)] + [anywhere] * 6,
         out_specs=(vmem, vmem),
         scratch_shapes=[
             pltpu.VMEM((SUBS + 1, held, species, width), f32),
@@ -320,6 +326,8 @@
             pltpu.VMEM(((1 + 2 * pairs) * species, 2 * species), jnp.bfloat16),
             dma((rows,)),
             dma((4,)),
+            pltpu.SMEM((1,), jnp.int32),
+            dma,
             dma,
             dma((2, SUBS)),
             dma((2, SUBS)),

time: 27.2 us -> 27.6 us (1.015)
  Pallas kernels: 25.8 us -> 26.1 us
    pallas_call x1, Pallas kernels: 24.7 us -> 25 us  [on_device(): pl.pallas_call(functools.partial(kernel, sizes), out_shape=(pltpu.VMEM((r...]
where the time goes in v5:
time: 27.6 us; the launch traced here: 27.4 us
  Pallas kernels  26.1 us (95%)
  between operations  1.29 us (5%)
    pallas_call x1, Pallas kernels, on_device(): pl.pallas_call(functools.partial(kernel, sizes), out_shape=(pltpu.VMEM((r...  25 us
    pallas_call x1, Pallas kernels, on_device(): pl.pallas_call(finish, out_shape=(jax.ShapeDtypeStruct(tracers.shape, f32...  1.11 us

profile of v5, /device:TPU:0, one launch (start us, length us, event | category | flops | bytes accessed | tf_op | source)
XLA Modules:
  0.0 27.4 jit_solution(14318858014180170546)
XLA Ops:
  1.3 25.0 %shard_map.86 = (f32[16,128,128]{2,1,0:T(8,128)S(1)}, f32[2,16,128]{2,1,0:T(8,128)S(1)}) custom-call(s32[1]{0:T(128)S(6)} %copy.9.count_ref, f32[128,16,128]{2,1,0:T(8,128)} %tracers.1, f32[2,16,128]{2,1,0:T(8,128)} %winds.1, f32[128,128]{1,0:T(8,128)} %linear.1, f32[1,128]{1,0:T(1,128)} %bitcast.1, f32[4,128,128]{2,1,0:T(8,128)} %left.1, f32[4,128,128]{2,1,0:T(8,128)} %right.1), custom_call_target="tpu_custom_call" | custom-call | tf_op jit(solution)/shard_map/pallas_call | solution.py:311
  26.3 1.1 %shard_map.87 = (f32[128,16,128]{2,1,0:T(8,128)}, f32[2,16,128]{2,1,0:T(8,128)}) custom-call(f32[16,128,128]{2,1,0:T(8,128)S(1)} %get-tuple-element.4.done, f32[2,16,128]{2,1,0:T(8,128)S(1)} %get-tuple-element.5.wind_new), custom_call_target="tpu_custom_call" | custom-call | tf_op jit(solution)/shard_map/pallas_call | solution.py:339
